TPU v7x, 32 devices: a whole 2x2x4 slice. The times are simulated.
32 devices in a mesh: freq: 8 (over y, x, core), rcv: 4 (over z).
Axes of the slice: x: 2, y: 2, z: 4, core: 2. Of those that a mesh axis runs over, the one named last changes fastest.
Arguments:
- green_freq: float32 [2, 8, 2304, 2304], P(None, 'freq', 'rcv'), may hold values from -6 to 6
- data_matrix: float32 [2, 8, 2304, 2304], P(None, 'freq', 'rcv'), may hold values from -0.09375 to 0.09375
- shot_panels: float32 [2, 8, 2304, 256], P(None, 'freq', 'rcv'), may hold values from -6 to 6
- wavelet: float32 [2, 8], P(None, 'freq'), may hold values from -1.5 to 1.5
- sources: int32 [256], replicated, may hold values from 0 to 2303, as said below
- support: int32 [8, 2304], replicated, may hold values 0 or 1
- threshold: float32 [1], replicated, may hold values from 3 to 7
Outputs:
- green_next: float32 [2, 8, 2304, 2304], P(None, 'freq', 'rcv')
- residual: float32 [2, 8, 2304, 256], P(None, 'freq', 'rcv')
Inputs may be any that keep to these rules, and one draw needn't show every extreme that they name: `sources`: 256 distinct source positions. `support`: a 0/1 mask over time samples and source positions.
All inputs are finite; a program needn't handle non-finite values.
Results may differ from a plain program's by a relative error of at most 0.00013.
Values sent between devices are 32-bit elements; how exact they have to be, the bound alone decides.
A program may use at most 128 MiB of HBM per device.

v0:
```python
import math
import jax
import jax.numpy as jnp
from jax import lax
from jax.sharding import PartitionSpec as P

HIGHEST = lax.Precision.HIGHEST


def complex_product(left_pair, right_pair, pattern):
    left_real, left_imag = left_pair
    right_real, right_imag = right_pair
    real_part = jnp.einsum(pattern, left_real, right_real, precision=HIGHEST) - jnp.einsum(
        pattern, left_imag, right_imag, precision=HIGHEST
    )
    imag_part = jnp.einsum(pattern, left_real, right_imag, precision=HIGHEST) + jnp.einsum(
        pattern, left_imag, right_real, precision=HIGHEST
    )
    return (real_part, imag_part)


def conj_product(left_pair, right_pair, pattern):
    left_real, left_imag = left_pair
    right_real, right_imag = right_pair
    real_part = jnp.einsum(pattern, left_real, right_real, precision=HIGHEST) + jnp.einsum(
        pattern, left_imag, right_imag, precision=HIGHEST
    )
    imag_part = jnp.einsum(pattern, left_real, right_imag, precision=HIGHEST) - jnp.einsum(
        pattern, left_imag, right_real, precision=HIGHEST
    )
    return (real_part, imag_part)


def shrink_spectra(spectra, keep, shrink_level):
    n_freq = spectra.shape[1]
    grid = jnp.arange(n_freq, dtype=jnp.int32)
    phase = grid[:, None] * grid[None, :] % n_freq
    angle = phase.astype(jnp.float32) * (2.0 * math.pi / n_freq)
    cos_table = jnp.cos(angle)
    sin_table = jnp.sin(angle)
    pattern = "tf,f...->t..."
    time_real = jnp.einsum(pattern, cos_table, spectra[0], precision=HIGHEST) - jnp.einsum(
        pattern, sin_table, spectra[1], precision=HIGHEST
    )
    time_imag = jnp.einsum(pattern, sin_table, spectra[0], precision=HIGHEST) + jnp.einsum(
        pattern, cos_table, spectra[1], precision=HIGHEST
    )
    magnitude = jnp.sqrt(time_real * time_real + time_imag * time_imag)
    factor = (
        jnp.maximum(magnitude - shrink_level, 0.0) / jnp.maximum(magnitude, shrink_level) * keep
    )
    kept_real = factor * time_real
    kept_imag = factor * time_imag
    back_real = (
        jnp.einsum(pattern, cos_table, kept_real, precision=HIGHEST)
        + jnp.einsum(pattern, sin_table, kept_imag, precision=HIGHEST)
    ) / n_freq
    back_imag = (
        jnp.einsum(pattern, cos_table, kept_imag, precision=HIGHEST)
        - jnp.einsum(pattern, sin_table, kept_real, precision=HIGHEST)
    ) / n_freq
    return jnp.stack([back_real, back_imag])


def on_device(green_freq, data_matrix, shot_panels, wavelet, sources, support, threshold):
    data_pair = (data_matrix[0], data_matrix[1])
    picked = jnp.take(green_freq, sources, axis=3)
    wave_real = wavelet[0][:, None, None]
    wave_imag = wavelet[1][:, None, None]
    rows_here = green_freq.shape[2]
    shard_piece = lax.all_gather(picked, "rcv", axis=2, tiled=True)
    block_real = data_matrix[0]
    block_imag = data_matrix[1]
    real_part, imag_part = complex_product(
        (block_real, block_imag), (shard_piece[0], shard_piece[1]), "frk,fkc->frc"
    )
    multiple = jnp.stack([real_part, imag_part])
    resid_real = shot_panels[0] - (wave_real * picked[0] - wave_imag * picked[1] - multiple[0])
    resid_imag = shot_panels[1] - (wave_real * picked[1] + wave_imag * picked[0] - multiple[1])
    residual = jnp.stack([resid_real, resid_imag])
    local_real = wave_real * resid_real + wave_imag * resid_imag
    local_imag = wave_real * resid_imag - wave_imag * resid_real
    adj_real, adj_imag = conj_product(data_pair, (resid_real, resid_imag), "frk,frc->kfc")
    summed_terms = -jnp.stack([adj_real, adj_imag], axis=1)
    own_rows = jnp.transpose(jnp.stack([local_real, local_imag]), (2, 0, 1, 3))
    row_offset = lax.axis_index("rcv") * rows_here
    summed_terms = summed_terms + lax.dynamic_update_slice_in_dim(
        jnp.zeros_like(summed_terms), own_rows, row_offset, 0
    )
    summed_all = lax.psum(summed_terms, "rcv")
    mine = lax.dynamic_slice_in_dim(summed_all, row_offset, rows_here, 0)
    direction = jnp.transpose(mine, (1, 2, 0, 3))
    push_real, push_imag = complex_product(
        data_pair, (summed_all[:, 0], summed_all[:, 1]), "frk,kfc->frc"
    )
    pushed = jnp.stack([push_real, push_imag])
    image_real = wave_real * direction[0] - wave_imag * direction[1] - pushed[0]
    image_imag = wave_real * direction[1] + wave_imag * direction[0] - pushed[1]
    norm_dir = jnp.sum(direction * direction)
    norm_img = jnp.sum(image_real * image_real + image_imag * image_imag)
    totals = lax.psum((norm_dir, norm_img), ("freq", "rcv"))
    step_size = totals[0] / totals[1]
    updated = green_freq.at[:, :, :, sources].add(step_size * direction)
    keep_all = support.astype(jnp.float32)
    gathered = lax.all_to_all(updated, "freq", split_axis=2, concat_axis=1, tiled=True)
    shrunk = shrink_spectra(gathered, keep_all[:, None, :], threshold[0])
    green_next = lax.all_to_all(shrunk, "freq", split_axis=1, concat_axis=2, tiled=True)
    return (green_next, residual)


def solution(mesh):
    in_specs = (
        P(None, "freq", "rcv", None),
        P(None, "freq", "rcv", None),
        P(None, "freq", "rcv", None),
        P(None, "freq"),
        P(),
        P(),
        P(),
    )
    out_specs = (P(None, "freq", "rcv", None), P(None, "freq", "rcv", None))
    return jax.shard_map(
        on_device, mesh=mesh, in_specs=in_specs, out_specs=out_specs, check_vma=False
    )
```

profile of v0, /device:TPU:0, one launch (start us, length us, event | category | flops | bytes accessed | tf_op | source)
XLA Modules:
  0.0 851.4 jit_solution(611839117997585425)
XLA Ops:
  8.6 19.2 %copy.30 = f32[2,1,576,2304]{2,0,3,1:T(2,128)} copy(f32[2,1,576,2304]{3,2,1,0:T(8,128)} %param.7) | data formatting | bytes 21233664 | tf_op args[0]
  37.8 91.2 %all-gather.2.cloned.1.call-done = f32[2,1,2304,256]{3,2,1,0:T(8,128)} async-done(((f32[2,1,576,256]{3,2,1,0:T(8,128)}), f32[2,1,2304,256]{3,2,1,0:T(8,128)}) %all-gather.2.cloned.1.call-update) | async-done | bytes 4718608 | tf_op jit(solution)/shard_map/all_gather | solution.py:71
  129.0 7.5 fusion.8
  136.6 9.7 %fusion.101 = f32[576,256]{1,0:T(8,128)S(1)} fusion(f32[256,576]{0,1:T(8,128)S(1)} %fusion.8, f32[2,1,576,2304]{3,2,1,0:T(8,128)} %param.8, f32[2,1,2304,256]{3,2,1,0:T(8,128)} %all-gather.2.cloned.1.call-done, f32[2,1,576,256]{3,2,1,0:T(8,128)} %param.9, f32[2,1,576,256]{3,2,1,0:T(8,128)S(1)} %copy-done.2, f32[]{:T(128)} %bitcast.6, f32[]{:T(128)} %bitcast.3), kind=kOutput, calls=%fused_computation.76 | convolution fusion | flops 4077748224 | bytes 10617856 | tf_op jit(solution)/shard_map/frk,fkc->frc/dot_general | solution.py:16
  146.3 11.9 %fusion.6 = f32[256,2304]{0,1:T(8,128)S(1)} fusion(f32[576,256]{1,0:T(8,128)S(1)} %fusion.101, f32[2,1,576,2304]{3,2,1,0:T(8,128)} %param.8), kind=kOutput, calls=%fused_computation.9 | convolution fusion | flops 4076863488 | bytes 8257536 | tf_op jit(solution)/shard_map/frk,frc->kfc/dot_general | solution.py:25
  168.3 9.6 %fusion.4 = f32[256,2304]{0,1:T(8,128)S(1)} fusion(f32[576,256]{1,0:T(8,128)S(1)} %fusion.98, f32[2,1,576,2304]{3,2,1,0:T(8,128)S(1)} %bitcast.238), kind=kOutput, calls=%fused_computation.7 | convolution fusion | flops 4076863488 | bytes 8257536 | tf_op jit(solution)/shard_map/frk,frc->kfc/dot_general | solution.py:28
  179.3 9.7 %fusion.41 = f32[2304,1,1,256]{3,0,2,1:T(8,128)S(1)} fusion(f32[256,2304]{0,1:T(8,128)S(1)} %fusion.6, f32[576,256]{1,0:T(8,128)S(1)} %fusion.98, f32[2,1,576,2304]{3,2,1,0:T(8,128)S(1)} %bitcast.238), kind=kOutput, calls=%fused_computation.44 | convolution fusion | flops 4077453312 | bytes 10616832 | tf_op jit(solution)/shard_map/frk,frc->kfc/dot_general | solution.py:25
  189.0 9.9 %fusion.38 = f32[2304,1,1,256]{3,0,2,1:T(8,128)S(1)} fusion(f32[256,2304]{0,1:T(8,128)S(1)} %fusion.4, f32[576,256]{1,0:T(8,128)S(1)} %fusion.101, f32[2,1,576,2304]{3,2,1,0:T(8,128)S(1)} %bitcast.238), kind=kOutput, calls=%fused_computation.43 | convolution fusion | flops 4077453312 | bytes 10616832 | tf_op jit(solution)/shard_map/frk,frc->kfc/dot_general | solution.py:28
  203.8 170.5 %all-reduce.3.cloned.1.call-done = f32[2304,2,1,256]{3,0,2,1:T(8,128)} async-done(((f32[2304,2,1,256]{3,0,2,1:T(8,128)}), f32[2304,2,1,256]{3,0,2,1:T(8,128)}) %all-reduce.3.cloned.1.call-update) | async-done | bytes 4718608 | tf_op jit(solution)/shard_map/psum | solution.py:90
  376.7 7.8 fusion
  403.5 39.4 %all-reduce = (f32[]{:T(128)}, f32[]{:T(128)}) all-reduce(f32[]{:T(128)} %get-tuple-element.8, f32[]{:T(128)} %fusion.109), channel_id=1, replica_groups=mesh['freq'=8,'rcv'=4] {'freq','rcv'}, use_global_device_ids=true, to_apply=%region_2.3 | all-reduce | flops 2 | bytes 16 | tf_op jit(solution)/shard_map/psum | solution.py:101
  449.2 31.0 %scatter_fusion = f32[2,576,2304]{1,0,2:T(2,128)} fusion(f32[2,576,2304]{1,0,2:T(2,128)} %bitcast.242, s32[256]{0:T(256)S(1)} %compare_select_fusion, f32[256,2,576]{2,1,0:T(2,128)S(1)} %copy.36), kind=kCustom, calls=%fused_computation.1 | custom fusion | flops 294912 | bytes 3539968 | tf_op jit(solution)/shard_map/scatter-add | solution.py:103
  480.3 21.2 %copy.37 = f32[2,1,576,2304]{3,0,1,2:T(2,128)} copy(f32[2,1,576,2304]{2,0,3,1:T(2,128)} %bitcast.243) | data formatting | bytes 21233664 | tf_op jit(solution)/shard_map/scatter-add | solution.py:103
  507.5 117.2 %all-to-all-done = f32[2,1,576,2304]{3,0,1,2:T(2,128)} async-done(((f32[2,1,576,2304]{3,0,1,2:T(2,128)}), f32[2,1,576,2304]{3,0,1,2:T(2,128)}, u32[]{:S(2)}, u32[]{:S(2)}) %all-to-all-start) | async-done | bytes 10616864 | tf_op jit(solution)/shard_map/all_to_all | solution.py:105
  624.7 12.6 %fusion.174 = (f32[1,1,576,2304]{3,0,1,2:T(1,128)S(1)}, f32[1,1,576,2304]{3,0,1,2:T(1,128)S(1)}) fusion(f32[2,1,576,2304]{3,0,1,2:T(2,128)} %all-to-all-done), kind=kLoop, calls=%fused_computation.145 | loop fusion | bytes 21233664 | tf_op jit(solution)/shard_map/slice | solution.py:43
  652.1 7.1 convolution_subtract_fusion
  659.2 7.4 convolution_add_fusion
  666.6 7.6 fusion.121
  674.3 8.0 fusion.119
  682.3 8.8 %multiply_bitcast_fusion.1 = f32[1,8,72,2304]{3,1,2,0:T(8,128)} fusion(f32[8,72,2304]{2,0,1:T(8,128)S(1)} %fusion.121, f32[8,72,2304]{2,0,1:T(8,128)S(1)} %convolution_add_fusion, f32[8,72,2304]{2,0,1:T(8,128)S(1)} %convolution_subtract_fusion, f32[8,2304]{1,0:T(8,128)S(1)} %convert_element_type.21, f32[]{:T(128)} %bitcast.234), kind=kOutput, calls=%fused_computation.28 | convolution fusion | flops 142001024 | bytes 21307396 | tf_op jit(solution)/shard_map/tf,f...->t.../dot_general | solution.py:56
  691.1 9.0 %multiply_bitcast_fusion = f32[1,8,72,2304]{3,1,2,0:T(8,128)} fusion(f32[8,72,2304]{2,0,1:T(8,128)S(1)} %fusion.119, f32[8,72,2304]{2,0,1:T(8,128)S(1)} %convolution_subtract_fusion, f32[8,72,2304]{2,0,1:T(8,128)S(1)} %convolution_add_fusion, f32[8,2304]{1,0:T(8,128)S(1)} %convert_element_type.21, f32[]{:T(128)} %bitcast.235), kind=kOutput, calls=%fused_computation.27 | convolution fusion | flops 142001024 | bytes 21307396 | tf_op jit(solution)/shard_map/tf,f...->t.../dot_general | solution.py:60
  704.9 7.4 copy.44
  718.5 116.8 %all-to-all-done.1 = f32[2,8,72,2304]{3,2,0,1:T(8,128)} async-done(((f32[2,8,72,2304]{3,2,0,1:T(8,128)}), f32[2,8,72,2304]{3,2,0,1:T(8,128)}, u32[]{:S(2)}, u32[]{:S(2)}) %all-to-all-start.1) | async-done | bytes 10616864 | tf_op jit(solution)/shard_map/all_to_all | solution.py:107
  835.3 9.0 %copy.45 = f32[2,8,72,2304]{3,2,1,0:T(8,128)} copy(f32[2,8,72,2304]{3,2,0,1:T(8,128)} %all-to-all-done.1) | data formatting | bytes 21233664 | tf_op jit(solution)/shard_map/all_to_all | solution.py:107
  (62 shorter events, 85.0 us)
Async XLA Ops:
  7.2 121.9 %all-gather.2.cloned.1.call-start = ((), (), s32[]{:S(2)}) async-start(), calls=%async_computation.2 | async-start | bytes 5898240 | tf_op jit(solution)/shard_map/all_gather | solution.py:71
  27.8 9.3 %copy-start.5 = (f32[2,1]{0,1:T(1,128)S(1)}, f32[2,1]{0,1:T(1,128)}, u32[]{:S(2)}) copy-start(f32[2,1]{0,1:T(1,128)} %param.10) | copy-start | bytes 28
  36.7 99.8 %copy-start.2 = (f32[2,1,576,256]{3,2,1,0:T(8,128)S(1)}, f32[2,1,576,256]{3,2,1,0:T(8,128)}, u32[]{:S(2)}) copy-start(f32[2,1,576,256]{3,2,1,0:T(8,128)} %bitcast_select_fusion) | copy-start | bytes 3538948
  36.8 337.6 %all-reduce.3.cloned.1.call-start = ((), (), s32[]{:S(2)}) async-start(), calls=%async_computation.3 | async-start | bytes 9437184 | tf_op jit(solution)/shard_map/psum | solution.py:90
  129.0 29.2 %slice-start = ((s8[10616832]{0:T(1024)(128)(4,1)}), s8[4194304]{0:T(1024)(128)(4,1)S(1)}, s32[]{:S(2)}) async-start(s8[10616832]{0:T(1024)(128)(4,1)} %bitcast.237), calls=%async_computation.4 | async-start | bytes 8388608
  129.0 29.2 %slice-start.6 = ((s8[4718592]{0:T(1024)(128)(4,1)}), s8[4194304]{0:T(1024)(128)(4,1)S(1)}, s32[]{:S(2)}) async-start(s8[4718592]{0:T(1024)(128)(4,1)} %bitcast.248), calls=%async_computation.10 | async-start | bytes 8388608
  136.5 21.7 %slice-start.1 = ((s8[10616832]{0:T(1024)(128)(4,1)}), s8[4194304]{0:T(1024)(128)(4,1)S(1)}, s32[]{:S(2)}) async-start(s8[10616832]{0:T(1024)(128)(4,1)} %bitcast.237), calls=%async_computation.5 | async-start | bytes 8388608
  136.5 21.7 %slice-start.2 = ((s8[10616832]{0:T(1024)(128)(4,1)}), s8[2228224]{0:T(1024)(128)(4,1)S(1)}, s32[]{:S(2)}) async-start(s8[10616832]{0:T(1024)(128)(4,1)} %bitcast.237), calls=%async_computation.6 | async-start | bytes 4456448
  136.5 21.7 %slice-start.7 = ((s8[4718592]{0:T(1024)(128)(4,1)}), s8[524288]{0:T(1024)(128)(4,1)S(1)}, s32[]{:S(2)}) async-start(s8[4718592]{0:T(1024)(128)(4,1)} %bitcast.248), calls=%async_computation.11 | async-start | bytes 1048576
  158.2 4.4 copy-start.3
  203.8 187.7 %slice-start.3 = ((s8[10616832]{0:T(1024)(128)(4,1)}), s8[2228224]{0:T(1024)(128)(4,1)S(1)}, s32[]{:S(2)}) async-start(s8[10616832]{0:T(1024)(128)(4,1)} %bitcast.239), calls=%async_computation.7 | async-start | bytes 4456448
  374.4 10.2 %copy-start = (f32[2304,2,1,256]{3,0,2,1:T(8,128)S(1)}, f32[2304,2,1,256]{3,0,2,1:T(8,128)}, u32[]{:S(2)}) copy-start(f32[2304,2,1,256]{3,0,2,1:T(8,128)} %all-reduce.3.cloned.1.call-done) | copy-start | bytes 14155780
  376.7 20.5 %copy-start.1 = (f32[2,1,576,256]{3,2,1,0:T(8,128)}, f32[2,1,576,256]{3,2,1,0:T(8,128)S(1)}, u32[]{:S(2)}) copy-start(f32[2,1,576,256]{3,2,1,0:T(8,128)S(1)} %get-tuple-element.9) | copy-start | bytes 3538948
  376.7 14.8 %slice-start.4 = ((s8[10616832]{0:T(1024)(128)(4,1)}), s8[4194304]{0:T(1024)(128)(4,1)S(1)}, s32[]{:S(2)}) async-start(s8[10616832]{0:T(1024)(128)(4,1)} %bitcast.239), calls=%async_computation.8 | async-start | bytes 8388608
  384.5 7.0 slice-start.5
  501.5 5.3 copy-start.4
  501.5 123.2 %all-to-all-start = ((f32[2,1,576,2304]{3,0,1,2:T(2,128)}), f32[2,1,576,2304]{3,0,1,2:T(2,128)}, u32[]{:S(2)}, u32[]{:S(2)}) async-start(f32[2,1,576,2304]{3,0,1,2:T(2,128)} %copy.37), calls=%async_computation | async-start | bytes 21233664 | tf_op jit(solution)/shard_map/all_to_all | solution.py:105
  712.2 123.1 %all-to-all-start.1 = ((f32[2,8,72,2304]{3,2,0,1:T(8,128)}), f32[2,8,72,2304]{3,2,0,1:T(8,128)}, u32[]{:S(2)}, u32[]{:S(2)}) async-start(f32[2,8,72,2304]{3,2,0,1:T(8,128)} %copy.44), calls=%async_computation.1 | async-start | bytes 21233664 | tf_op jit(solution)/shard_map/all_to_all | solution.py:107
Sparse Core Ops, SparseCore 0:
  36.9 92.0 all-gather.1
  203.9 170.3 all-reduce.2
where the time goes:
time: 856 us; the launch traced here: 851 us
  waiting for transfers between devices  496 us (58%)
  matrix products  157 us (18%)
  local copies, waits for them, and re-layouts  81.3 us (9%)
  other arithmetic  50.4 us (6%)
  blocking collectives  39.4 us (5%)
  between operations  16.6 us (2%)
  starting transfers between devices  10.8 us (1%)
    psum x1, waiting for transfers between devices, on_device(): summed_all = lax.psum(summed_terms, 'rcv')  171 us
    all_to_all x1, waiting for transfers between devices, on_device(): lax.all_to_all(updated, 'freq', split_axis=2, concat_axis=1, tiled=True)  117 us
    all_to_all x1, waiting for transfers between devices, on_device(): lax.all_to_all(shrunk, 'freq', split_axis=1, concat_axis=2, tiled=True)  117 us
    all_gather x1, waiting for transfers between devices, on_device(): shard_piece = lax.all_gather(picked, 'rcv', axis=2, tiled=True)  91.2 us
    psum x1, blocking collectives, on_device(): totals = lax.psum((norm_dir, norm_img), ('freq', 'rcv'))  39.4 us
    scatter-add x1, other arithmetic, on_device(): updated = green_freq.at[:, :, :, sources].add(step_size * direction)  31 us
    scatter-add x1, local copies, waits for them, and re-layouts, on_device(): updated = green_freq.at[:, :, :, sources].add(step_size * direction)  21.2 us
    unnamed x31, local copies, waits for them, and re-layouts  20 us
  transfers between devices with their start and end apart: 4, of which 4 were waited for; matrix products, arithmetic and copies ran while one was open for 0% of the time, Pallas kernels for 0%

commit v1 on v0

--- a/solution.py
+++ b/solution.py
@@ -68,7 +68,12 @@
     wave_real = wavelet[0][:, None, None]
     wave_imag = wavelet[1][:, None, None]
     rows_here = green_freq.shape[2]
-    shard_piece = lax.all_gather(picked, "rcv", axis=2, tiled=True)
+    ring = [picked]
+    for hop in range(3):
+        ring.append(lax.ppermute(ring[-1], "rcv", [(dev, (dev + 1) % 4) for dev in range(4)]))
+    shard_piece = jnp.roll(
+        jnp.concatenate(ring[::-1], axis=2), (lax.axis_index("rcv") + 1) * ring[0].shape[2], axis=2
+    )
     block_real = data_matrix[0]
     block_imag = data_matrix[1]
     real_part, imag_part = complex_product(

time: 856 us -> 851 us (level)
    all_gather x1 -> x0, waiting for transfers between devices: 91.2 us -> none  [on_device(): shard_piece = lax.all_gather(picked, 'rcv', axis=2, tiled=True)]
    ppermute x0 -> x3, waiting for transfers between devices: none -> 84.8 us  [on_device(): lax.ppermute(ring[-1], 'rcv', [(dev, (dev + 1) % 4) for dev in range(4)])]
    unnamed x31 -> x39, local copies, waits for them, and re-layouts: 20 us -> 26.9 us
  transfers between devices with their start and end apart: 4 -> 6, of which waited for: 4 -> 6; matrix products, arithmetic and copies ran while one was open for 0% -> 0% of each run, Pallas kernels for 0% -> 0%
where the time goes in v1:
time: 851 us; the launch traced here: 845 us
  waiting for transfers between devices  489 us (57%)
  matrix products  149 us (18%)
  local copies, waits for them, and re-layouts  87.5 us (10%)
  other arithmetic  49.6 us (6%)
  blocking collectives  39.4 us (5%)
  between operations  16.8 us (2%)
  starting transfers between devices  14.1 us (2%)
    psum x1, waiting for transfers between devices, on_device(): summed_all = lax.psum(summed_terms, 'rcv')  170 us
    all_to_all x1, waiting for transfers between devices, on_device(): lax.all_to_all(updated, 'freq', split_axis=2, concat_axis=1, tiled=True)  117 us
    all_to_all x1, waiting for transfers between devices, on_device(): lax.all_to_all(shrunk, 'freq', split_axis=1, concat_axis=2, tiled=True)  117 us
    ppermute x3, waiting for transfers between devices, on_device(): lax.ppermute(ring[-1], 'rcv', [(dev, (dev + 1) % 4) for dev in range(4)])  84.8 us
    psum x1, blocking collectives, on_device(): totals = lax.psum((norm_dir, norm_img), ('freq', 'rcv'))  39.4 us
    scatter-add x1, other arithmetic, on_device(): updated = green_freq.at[:, :, :, sources].add(step_size * direction)  31 us
    unnamed x39, local copies, waits for them, and re-layouts  26.9 us
    scatter-add x1, local copies, waits for them, and re-layouts, on_device(): updated = green_freq.at[:, :, :, sources].add(step_size * direction)  21.2 us
  transfers between devices with their start and end apart: 6, of which 6 were waited for; matrix products, arithmetic and copies ran while one was open for 0% of the time, Pallas kernels for 0%

profile of v1, /device:TPU:0, one launch (start us, length us, event | category | flops | bytes accessed | tf_op | source)
XLA Modules:
  0.0 845.3 jit_solution(4104606612418833740)
XLA Ops:
  8.6 19.2 %copy.30 = f32[2,1,576,2304]{2,0,3,1:T(2,128)} copy(f32[2,1,576,2304]{3,2,1,0:T(8,128)} %param.7) | data formatting | bytes 21233664 | tf_op args[0]
  38.8 28.0 %collective-permute-done = f32[2,1,576,256]{3,2,1,0:T(8,128)S(1)} collective-permute-done((f32[2,1,576,256]{3,2,1,0:T(8,128)S(1)}, f32[2,1,576,256]{3,2,1,0:T(8,128)S(1)}, u32[]{:S(2)}, u32[]{:S(2)}) %collective-permute-start) | collective-permute-done | bytes 1179680 | tf_op jit(solution)/shard_map/ppermute | solution.py:73
  67.9 29.0 %collective-permute-done.1 = f32[2,1,576,256]{3,2,1,0:T(8,128)} collective-permute-done((f32[2,1,576,256]{3,2,1,0:T(8,128)S(1)}, f32[2,1,576,256]{3,2,1,0:T(8,128)}, u32[]{:S(2)}, u32[]{:S(2)}) %collective-permute-start.1) | collective-permute-done | bytes 1179680 | tf_op jit(solution)/shard_map/ppermute | solution.py:73
  98.0 27.7 %collective-permute-done.2 = f32[2,1,576,256]{3,2,1,0:T(8,128)} collective-permute-done((f32[2,1,576,256]{3,2,1,0:T(8,128)}, f32[2,1,576,256]{3,2,1,0:T(8,128)}, u32[]{:S(2)}, u32[]{:S(2)}) %collective-permute-start.2) | collective-permute-done | bytes 1179680 | tf_op jit(solution)/shard_map/ppermute | solution.py:73
  152.3 10.3 %fusion.6 = f32[256,2304]{0,1:T(8,128)S(1)} fusion(f32[576,256]{1,0:T(8,128)S(1)} %fusion.101, f32[2,1,576,2304]{3,2,1,0:T(8,128)S(1)} %bitcast.242), kind=kOutput, calls=%fused_computation.9 | convolution fusion | flops 4076863488 | bytes 8257536 | tf_op jit(solution)/shard_map/frk,frc->kfc/dot_general | solution.py:25
  163.9 10.5 %fusion.4 = f32[256,2304]{0,1:T(8,128)S(1)} fusion(f32[576,256]{1,0:T(8,128)S(1)} %fusion.98, f32[2,1,576,2304]{3,2,1,0:T(8,128)S(1)} %bitcast.242), kind=kOutput, calls=%fused_computation.7 | convolution fusion | flops 4076863488 | bytes 8257536 | tf_op jit(solution)/shard_map/frk,frc->kfc/dot_general | solution.py:28
  174.4 9.5 %fusion.41 = f32[2304,1,1,256]{3,0,2,1:T(8,128)S(1)} fusion(f32[256,2304]{0,1:T(8,128)S(1)} %fusion.6, f32[576,256]{1,0:T(8,128)S(1)} %fusion.98, f32[2,1,576,2304]{3,2,1,0:T(8,128)S(1)} %bitcast.242), kind=kOutput, calls=%fused_computation.44 | convolution fusion | flops 4077453312 | bytes 10616832 | tf_op jit(solution)/shard_map/frk,frc->kfc/dot_general | solution.py:25
  184.0 9.7 %fusion.38 = f32[2304,1,1,256]{3,0,2,1:T(8,128)S(1)} fusion(f32[256,2304]{0,1:T(8,128)S(1)} %fusion.4, f32[576,256]{1,0:T(8,128)S(1)} %fusion.101, f32[2,1,576,2304]{3,2,1,0:T(8,128)S(1)} %bitcast.242), kind=kOutput, calls=%fused_computation.43 | convolution fusion | flops 4077453312 | bytes 10616832 | tf_op jit(solution)/shard_map/frk,frc->kfc/dot_general | solution.py:28
  198.7 169.9 %all-reduce.3.cloned.1.call-done = f32[2304,2,1,256]{3,0,2,1:T(8,128)} async-done(((f32[2304,2,1,256]{3,0,2,1:T(8,128)}), f32[2304,2,1,256]{3,0,2,1:T(8,128)}) %all-reduce.3.cloned.1.call-update) | async-done | bytes 4718608 | tf_op jit(solution)/shard_map/psum | solution.py:95
  370.9 7.8 fusion
  378.7 7.2 fusion.2
  397.9 39.4 %all-reduce = (f32[]{:T(128)}, f32[]{:T(128)}) all-reduce(f32[]{:T(128)} %get-tuple-element.8, f32[]{:T(128)} %fusion.109), channel_id=1, replica_groups=mesh['freq'=8,'rcv'=4] {'freq','rcv'}, use_global_device_ids=true, to_apply=%region_2.3 | all-reduce | flops 2 | bytes 16 | tf_op jit(solution)/shard_map/psum | solution.py:106
  443.7 31.0 %scatter_fusion = f32[2,576,2304]{1,0,2:T(2,128)} fusion(f32[2,576,2304]{1,0,2:T(2,128)} %bitcast.246, s32[256]{0:T(256)S(1)} %compare_select_fusion, f32[256,2,576]{2,1,0:T(2,128)S(1)} %copy.36), kind=kCustom, calls=%fused_computation.1 | custom fusion | flops 294912 | bytes 3539968 | tf_op jit(solution)/shard_map/scatter-add | solution.py:108
  474.8 21.2 %copy.37 = f32[2,1,576,2304]{3,0,1,2:T(2,128)} copy(f32[2,1,576,2304]{2,0,3,1:T(2,128)} %bitcast.247) | data formatting | bytes 21233664 | tf_op jit(solution)/shard_map/scatter-add | solution.py:108
  501.9 117.2 %all-to-all-done = f32[2,1,576,2304]{3,0,1,2:T(2,128)} async-done(((f32[2,1,576,2304]{3,0,1,2:T(2,128)}), f32[2,1,576,2304]{3,0,1,2:T(2,128)}, u32[]{:S(2)}, u32[]{:S(2)}) %all-to-all-start) | async-done | bytes 10616864 | tf_op jit(solution)/shard_map/all_to_all | solution.py:110
  619.2 12.0 %fusion.178 = (f32[1,1,576,2304]{3,0,1,2:T(1,128)S(1)}, f32[1,1,576,2304]{3,0,1,2:T(1,128)S(1)}) fusion(f32[2,1,576,2304]{3,0,1,2:T(2,128)} %all-to-all-done), kind=kLoop, calls=%fused_computation.157 | loop fusion | bytes 21233664 | tf_op jit(solution)/shard_map/slice | solution.py:43
  653.1 7.6 convolution_add_fusion
  660.7 7.6 fusion.121
  668.3 7.8 fusion.119
  676.1 8.9 %multiply_bitcast_fusion.1 = f32[1,8,72,2304]{3,1,2,0:T(8,128)} fusion(f32[8,72,2304]{2,0,1:T(8,128)S(1)} %fusion.121, f32[8,72,2304]{2,0,1:T(8,128)S(1)} %convolution_add_fusion, f32[8,72,2304]{2,0,1:T(8,128)S(1)} %convolution_subtract_fusion, f32[8,2304]{1,0:T(8,128)S(1)} %convert_element_type.21, f32[]{:T(128)} %bitcast.238), kind=kOutput, calls=%fused_computation.28 | convolution fusion | flops 142001024 | bytes 21307396 | tf_op jit(solution)/shard_map/tf,f...->t.../dot_general | solution.py:56
  685.0 9.0 %multiply_bitcast_fusion = f32[1,8,72,2304]{3,1,2,0:T(8,128)} fusion(f32[8,72,2304]{2,0,1:T(8,128)S(1)} %fusion.119, f32[8,72,2304]{2,0,1:T(8,128)S(1)} %convolution_subtract_fusion, f32[8,72,2304]{2,0,1:T(8,128)S(1)} %convolution_add_fusion, f32[8,2304]{1,0:T(8,128)S(1)} %convert_element_type.21, f32[]{:T(128)} %bitcast.239), kind=kOutput, calls=%fused_computation.27 | convolution fusion | flops 142001024 | bytes 21307396 | tf_op jit(solution)/shard_map/tf,f...->t.../dot_general | solution.py:60
  698.8 7.4 copy.44
  712.4 116.8 %all-to-all-done.1 = f32[2,8,72,2304]{3,2,0,1:T(8,128)} async-done(((f32[2,8,72,2304]{3,2,0,1:T(8,128)}), f32[2,8,72,2304]{3,2,0,1:T(8,128)}, u32[]{:S(2)}, u32[]{:S(2)}) %all-to-all-start.1) | async-done | bytes 10616864 | tf_op jit(solution)/shard_map/all_to_all | solution.py:112
  829.2 9.0 %copy.45 = f32[2,8,72,2304]{3,2,1,0:T(8,128)} copy(f32[2,8,72,2304]{3,2,0,1:T(8,128)} %all-to-all-done.1) | data formatting | bytes 21233664 | tf_op jit(solution)/shard_map/all_to_all | solution.py:112
  (74 shorter events, 104.7 us)
Async XLA Ops:
  7.2 361.4 %all-reduce.3.cloned.1.call-start = ((), (), s32[]{:S(2)}) async-start(), calls=%async_computation.2 | async-start | bytes 9437184 | tf_op jit(solution)/shard_map/psum | solution.py:95
  27.8 69.6 %copy-start.8 = (f32[2,1]{0,1:T(1,128)S(1)}, f32[2,1]{0,1:T(1,128)}, u32[]{:S(2)}) copy-start(f32[2,1]{0,1:T(1,128)} %param.10) | copy-start | bytes 28
  35.6 96.3 %slice-start = ((s8[10616832]{0:T(1024)(128)(4,1)}), s8[2228224]{0:T(1024)(128)(4,1)S(1)}, s32[]{:S(2)}) async-start(s8[10616832]{0:T(1024)(128)(4,1)} %bitcast.241), calls=%async_computation.3 | async-start | bytes 4456448
  35.7 61.2 %copy-start.4 = (f32[2,1,576,256]{3,2,1,0:T(8,128)}, f32[2,1,576,256]{3,2,1,0:T(8,128)S(1)}, u32[]{:S(2)}) copy-start(f32[2,1,576,256]{3,2,1,0:T(8,128)S(1)} %bitcast_select_fusion) | copy-start | bytes 3538948
  35.7 31.1 %collective-permute-start = (f32[2,1,576,256]{3,2,1,0:T(8,128)S(1)}, f32[2,1,576,256]{3,2,1,0:T(8,128)S(1)}, u32[]{:S(2)}, u32[]{:S(2)}) collective-permute-start(f32[2,1,576,256]{3,2,1,0:T(8,128)S(1)} %bitcast_select_fusion), channel_id=1, source_target_pairs={{0,1},{1,2},{2,3},{3,0},{4,5},{5,6},{6,7},{7,4},{8,9},{9,10},{10,1... | collective-permute-start | bytes 3538952 | tf_op jit(solution)/shard_map/ppermute | solution.py:73
  66.8 1.0 copy-start.2
  67.8 29.0 %collective-permute-start.1 = (f32[2,1,576,256]{3,2,1,0:T(8,128)S(1)}, f32[2,1,576,256]{3,2,1,0:T(8,128)}, u32[]{:S(2)}, u32[]{:S(2)}) collective-permute-start(f32[2,1,576,256]{3,2,1,0:T(8,128)S(1)} %collective-permute-done), channel_id=1, source_target_pairs={{0,1},{1,2},{2,3},{3,0},{4,5},{5,6},{6,7},{7,4},{8,9},{9,10},{10,1... | collective-permute-start | bytes 3538952 | tf_op jit(solution)/shard_map/ppermute | solution.py:73
  96.9 28.9 %collective-permute-start.2 = (f32[2,1,576,256]{3,2,1,0:T(8,128)}, f32[2,1,576,256]{3,2,1,0:T(8,128)}, u32[]{:S(2)}, u32[]{:S(2)}) collective-permute-start(f32[2,1,576,256]{3,2,1,0:T(8,128)} %collective-permute-done.1), channel_id=1, source_target_pairs={{0,1},{1,2},{2,3},{3,0},{4,5},{5,6},{6,7},{7,4},{8,9},{9,10},{10,1... | collective-permute-start | bytes 3538952 | tf_op jit(solution)/shard_map/ppermute | solution.py:73
  97.4 31.2 %copy-start.3 = (f32[2,1,576,256]{3,2,1,0:T(8,128)S(1)}, f32[2,1,576,256]{3,2,1,0:T(8,128)}, u32[]{:S(2)}) copy-start(f32[2,1,576,256]{3,2,1,0:T(8,128)} %copy-done.2) | copy-start | bytes 3538948
  127.1 4.8 slice-start.1
  128.9 3.1 slice-start.2
  136.4 4.4 copy-start.5
  136.4 4.4 copy-start.6
  198.6 187.3 %slice-start.3 = ((s8[10616832]{0:T(1024)(128)(4,1)}), s8[2228224]{0:T(1024)(128)(4,1)S(1)}, s32[]{:S(2)}) async-start(s8[10616832]{0:T(1024)(128)(4,1)} %bitcast.243), calls=%async_computation.6 | async-start | bytes 4456448
  368.5 10.2 %copy-start = (f32[2304,2,1,256]{3,0,2,1:T(8,128)S(1)}, f32[2304,2,1,256]{3,0,2,1:T(8,128)}, u32[]{:S(2)}) copy-start(f32[2304,2,1,256]{3,0,2,1:T(8,128)} %all-reduce.3.cloned.1.call-done) | copy-start | bytes 14155780
  370.9 20.7 %copy-start.1 = (f32[2,1,576,256]{3,2,1,0:T(8,128)}, f32[2,1,576,256]{3,2,1,0:T(8,128)S(1)}, u32[]{:S(2)}) copy-start(f32[2,1,576,256]{3,2,1,0:T(8,128)S(1)} %get-tuple-element.9) | copy-start | bytes 3538948
  370.9 15.1 %slice-start.4 = ((s8[10616832]{0:T(1024)(128)(4,1)}), s8[4194304]{0:T(1024)(128)(4,1)S(1)}, s32[]{:S(2)}) async-start(s8[10616832]{0:T(1024)(128)(4,1)} %bitcast.243), calls=%async_computation.7 | async-start | bytes 8388608
  378.7 7.2 slice-start.5
  496.0 5.3 copy-start.7
  496.0 123.2 %all-to-all-start = ((f32[2,1,576,2304]{3,0,1,2:T(2,128)}), f32[2,1,576,2304]{3,0,1,2:T(2,128)}, u32[]{:S(2)}, u32[]{:S(2)}) async-start(f32[2,1,576,2304]{3,0,1,2:T(2,128)} %copy.37), calls=%async_computation | async-start | bytes 21233664 | tf_op jit(solution)/shard_map/all_to_all | solution.py:110
  706.1 123.1 %all-to-all-start.1 = ((f32[2,8,72,2304]{3,2,0,1:T(8,128)}), f32[2,8,72,2304]{3,2,0,1:T(8,128)}, u32[]{:S(2)}, u32[]{:S(2)}) async-start(f32[2,8,72,2304]{3,2,0,1:T(8,128)} %copy.44), calls=%async_computation.1 | async-start | bytes 21233664 | tf_op jit(solution)/shard_map/all_to_all | solution.py:112
Sparse Core Ops, SparseCore 0:
  198.8 169.7 all-reduce.2
